TPU v7x, 512 devices: a whole 4x8x8 slice. The times are simulated.
512 devices in a mesh: geo: 128 (over y, z, core), deg: 4 (over x).
Axes of the slice: x: 4, y: 8, z: 8, core: 2. Of those that a mesh axis runs over, the one named last changes fastest.
Arguments:
- lo_ainv: bfloat16 [20, 20, 65536], P(None, None, ('geo', 'deg')), may hold values from -1.25 to 1.25
- lo_geom: float32 [12, 65536], P(None, ('geo', 'deg')), may hold values from -1.5 to 1.5
- lo_load: bfloat16 [20, 65536], P(None, ('geo', 'deg')), may hold values from -6 to 6
- lo_degree: int32 [65536], P(('geo', 'deg')), may hold values from 1 to 3, as said below
- lo_send: int32 [4, 65536], P(None, ('geo', 'deg')), may hold values from 0 to 767, as said below
- hi_geom: float32 [12, 65536], P(None, ('geo', 'deg')), may hold values from -1.5 to 1.5
- hi_load: bfloat16 [84, 65536], P(None, ('geo', 'deg')), may hold values from -6 to 6
- hi_degree: int32 [65536], P(('geo', 'deg')), may hold values from 0 to 6, as said below
- hi_slot: int32 [65536], P(('geo', 'deg')), may hold values from -1 to 127, as said below
- hi_ainv: bfloat16 [84, 84, 65536], P(None, None, ('geo', 'deg')), may hold values from -0.625 to 0.625
- hi_send: int32 [4, 65536], P(None, ('geo', 'deg')), may hold values from -1 to 767, as said below
- recv_face: int32 [786432], P(('geo', 'deg')), may hold values from -1 to 767, as said below
- lift_ref: float32 [4, 4, 28, 84], replicated, may hold values from -1.25 to 1.25
- trace_ref: float32 [4, 84, 4, 28], replicated, may hold values from -1.25 to 1.25
- face_mass: float32 [28, 28], replicated, may hold values from -2 to 2
Outputs:
- low_particular: float32 [20, 65536], P(None, ('geo', 'deg'))
- high_particular: float32 [84, 65536], P(None, ('geo', 'deg'))
- trace_blocks: float32 [28, 28, 393216], P(None, None, ('geo', 'deg'))
- trace_rhs: float32 [28, 393216], P(None, ('geo', 'deg'))
Inputs may be any that keep to these rules, and one draw needn't show every extreme that they name: `lo_degree`: every LOW position holds an element of degree 1, 2 or 3. `hi_degree`: 0 where the position holds no element, else 4, 5 or 6. `hi_slot`: -1 exactly where hi_degree is 0; the other values are distinct on a device, so at most 32 elements go from one device to one device of its deg group; in some geo index every batch slot is filled. `lo_send`: values are distinct on a device, so at most 6 rows go from one device to one owner; some owners receive 6 LOW rows from every device of their deg index. `hi_send`: -1 exactly for the faces of batch slots that receive no element; the other values are distinct on a device; some owners receive 6 HIGH rows from every device of their deg index. `recv_face`: -1 exactly where no row arrives; a face of a device is named at most twice among that device's entries.
All inputs are finite; a program needn't handle non-finite values.
Results may differ from a plain program's by a relative error of at most 0.0095.
Values may be sent and summed in bfloat16 or wider, within the bound.
A program may use at most 64 MiB of HBM per device.

v0:
```python
import jax
import jax.numpy as jnp
from jax import lax
from jax.sharding import PartitionSpec as P

NI_LO = 20
NF_LO = 10


def prefix_masks(degree_value, inner_width, face_width):
    inner_count = (degree_value + 1.0) * (degree_value + 2.0) * (degree_value + 3.0) / 6.0
    face_count = (degree_value + 1.0) * (degree_value + 2.0) / 2.0
    inner_mask = (
        jnp.arange(inner_width, dtype=jnp.float32)[:, None] < inner_count[None, :]
    ).astype(jnp.float32)
    face_mask = (jnp.arange(face_width, dtype=jnp.float32)[:, None] < face_count[None, :]).astype(
        jnp.float32
    )
    return (inner_mask, face_mask)


def condense(inverse, geometry, load_values, degree_value, lift_table, trace_table, mass_table):
    term_count = lift_table.shape[0]
    face_width = mass_table.shape[0]
    element_count = geometry.shape[1]
    inner_mask, face_mask = prefix_masks(degree_value, inverse.shape[0], face_width)
    lift_mix = jnp.einsum(
        "kaij,ke->aije", lift_table, geometry[:term_count], precision=lax.Precision.HIGHEST
    )
    lift_mat = (lift_mix * face_mask[None, :, None, :] * inner_mask[None, None, :, :]).astype(
        jnp.bfloat16
    )
    trace_mix = jnp.einsum(
        "kjai,ke->jaie",
        trace_table,
        geometry[term_count : 2 * term_count],
        precision=lax.Precision.HIGHEST,
    )
    trace_mat = (trace_mix * inner_mask[:, None, None, :] * face_mask[None, None, :, :]).astype(
        jnp.bfloat16
    )
    solved = jnp.einsum(
        "jle,laie->jaie", inverse, trace_mat, preferred_element_type=jnp.float32
    ).astype(jnp.bfloat16)
    coupling = jnp.einsum("aije,jame->imae", lift_mat, solved, preferred_element_type=jnp.float32)
    scaling = geometry[2 * term_count : 2 * term_count + 4]
    pair_mask = face_mask[:, None, :] * face_mask[None, :, :]
    schur_block = (
        mass_table[:, :, None, None] * scaling[None, None, :, :] * pair_mask[:, :, None, :]
        - coupling
    )
    masked_load = load_values * inner_mask.astype(jnp.bfloat16)
    particular = inner_mask * jnp.einsum(
        "jle,le->je", inverse, masked_load, preferred_element_type=jnp.float32
    )
    rhs_part = -jnp.einsum(
        "aije,je->iae",
        lift_mat,
        particular.astype(jnp.bfloat16),
        preferred_element_type=jnp.float32,
    )
    face_rows = jnp.concatenate(
        [
            schur_block.reshape(face_width * face_width, 4 * element_count),
            rhs_part.reshape(face_width, 4 * element_count),
        ],
        axis=0,
    )
    return (face_rows.astype(jnp.bfloat16), particular)


def fill_buffer(face_rows, positions, slot_total):
    target = jnp.where(positions < 0, slot_total, positions)
    empty_buffer = jnp.zeros((face_rows.shape[0], slot_total), face_rows.dtype)
    return empty_buffer.at[:, target].set(face_rows, mode="drop")


def embed_rows(face_rows, narrow, wide_face):
    row_count = face_rows.shape[1]
    block_part = face_rows[: narrow * narrow].reshape(narrow, narrow, row_count)
    block_part = jnp.pad(block_part, ((0, wide_face - narrow), (0, wide_face - narrow), (0, 0)))
    right_part = jnp.pad(face_rows[narrow * narrow :], ((0, wide_face - narrow), (0, 0)))
    return jnp.concatenate(
        [block_part.reshape(wide_face * wide_face, row_count), right_part], axis=0
    )


def accumulate(blocks, right_side, arrived_rows, receive_plan, narrow):
    face_total = blocks.shape[2]
    block_width = min(512, face_total)
    pieces = []
    begin = 0
    while begin < face_total:
        width_here = min(block_width, face_total - begin)
        columns = begin + jnp.arange(width_here, dtype=jnp.int32)
        selector = (receive_plan[:, None] == columns[None, :]).astype(jnp.bfloat16)
        pieces.append(jnp.dot(arrived_rows, selector, preferred_element_type=jnp.float32))
        begin = begin + width_here
    summed = jnp.concatenate(pieces, axis=1)
    block_part = summed[: narrow * narrow].reshape(narrow, narrow, face_total)
    blocks = blocks.at[:narrow, :narrow].add(block_part)
    right_side = right_side.at[:narrow].add(summed[narrow * narrow :])
    return (blocks, right_side)


def on_device(
    lo_ainv,
    lo_geom,
    lo_load,
    lo_degree,
    lo_send,
    hi_geom,
    hi_load,
    hi_degree,
    hi_slot,
    hi_ainv,
    hi_send,
    recv_face,
    lift_ref,
    trace_ref,
    face_mass,
):
    wide_face = face_mass.shape[0]
    inner_width = hi_ainv.shape[0]
    geo_rows = hi_geom.shape[0]
    low_rows, low_particular = condense(
        lo_ainv,
        lo_geom,
        lo_load,
        lo_degree.astype(jnp.float32),
        lift_ref[:, :, :NF_LO, :NI_LO],
        trace_ref[:, :NI_LO, :, :NF_LO],
        face_mass[:NF_LO, :NF_LO],
    )
    record = jnp.concatenate(
        [hi_geom, hi_load.astype(jnp.float32), hi_degree.astype(jnp.float32)[None, :]], axis=0
    )
    outgoing = fill_buffer(record, hi_slot, hi_slot.shape[0])
    arrived = lax.all_to_all(outgoing, "deg", split_axis=1, concat_axis=1, tiled=True)
    high_rows, high_particular = condense(
        hi_ainv,
        arrived[:geo_rows],
        arrived[geo_rows : geo_rows + inner_width].astype(jnp.bfloat16),
        arrived[geo_rows + inner_width],
        lift_ref,
        trace_ref,
        face_mass,
    )
    groups = lax.axis_size("geo")
    cap_low = max(2, 6 * lo_ainv.shape[2] // groups)
    cap_high = max(2, 6 * hi_ainv.shape[2] // groups)
    per_owner = cap_low + cap_high
    face_total = (groups * per_owner + 1) // 2
    blocks = jnp.zeros((wide_face, wide_face, face_total), jnp.float32)
    right_side = jnp.zeros((wide_face, face_total), jnp.float32)
    low_positions = lo_send.reshape(-1)
    high_positions = hi_send.reshape(-1)
    low_target = jnp.where(
        low_positions < 0, -1, low_positions // cap_low * per_owner + low_positions % cap_low
    )
    high_target = jnp.where(
        high_positions < 0,
        -1,
        high_positions // cap_high * per_owner + cap_low + high_positions % cap_high,
    )
    combined = jnp.concatenate([embed_rows(low_rows, NF_LO, wide_face), high_rows], axis=1)
    positions = jnp.concatenate([low_target, high_target])
    arrived_rows = lax.all_to_all(
        fill_buffer(combined, positions, groups * per_owner),
        "geo",
        split_axis=1,
        concat_axis=1,
        tiled=True,
    )
    blocks, right_side = accumulate(blocks, right_side, arrived_rows, recv_face, wide_face)
    return (low_particular, high_particular, blocks, right_side)


def solution(mesh):
    in_specs = (
        P(None, None, ("geo", "deg")),
        P(None, ("geo", "deg")),
        P(None, ("geo", "deg")),
        P(("geo", "deg")),
        P(None, ("geo", "deg")),
        P(None, ("geo", "deg")),
        P(None, ("geo", "deg")),
        P(("geo", "deg")),
        P(("geo", "deg")),
        P(None, None, ("geo", "deg")),
        P(None, ("geo", "deg")),
        P(("geo", "deg")),
        P(),
        P(),
        P(),
    )
    out_specs = (
        P(None, ("geo", "deg")),
        P(None, ("geo", "deg")),
        P(None, None, ("geo", "deg")),
        P(None, ("geo", "deg")),
    )
    return jax.shard_map(
        on_device, mesh=mesh, in_specs=in_specs, out_specs=out_specs, check_vma=False
    )
```

profile of v0, /device:TPU:27, one launch (start us, length us, event | category | flops | bytes accessed | tf_op | source)
XLA Modules:
  0.0 220.3 jit_solution(9106446782423416625)
XLA Ops:
  0.6 0.7 convert_element_type.120
  1.4 0.7 convert_bitcast_fusion
  2.0 0.7 maximum_bitcast_fusion
  2.7 0.1 copy.105
  2.8 0.7 compare_select_fusion.2
  3.5 1.5 scatter_custom_fusion
  5.0 4.3 %all-to-all-start = ((f32[97,4,32]{0,2,1:T(8,128)}), f32[97,4,32]{0,2,1:T(8,128)S(1)}, u32[]{:S(2)}, u32[]{:S(2)}) async-start(f32[97,4,32]{0,2,1:T(8,128)} %bitcast.9), calls=%async_computation | async-start | bytes 131072 | tf_op jit(solution)/shard_map/all_to_all | solution.py:139
  9.2 0.7 broadcast_multiply_fusion.2
  9.9 0.7 bitcast_convert_fusion.2
  10.6 2.2 copy.112
  12.8 1.0 multiply_reduce_fusion.2
  13.7 0.6 bitcast_convert_fusion.1
  14.4 1.0 copy.113
  15.4 0.1 copy.108
  15.5 1.7 multiply_reduce_fusion.1
  17.2 1.7 copy.114
  18.9 0.9 slice.92
  19.8 0.2 copy.167
  20.1 1.2 fusion.35
  21.3 2.7 %copy.111 = bf16[20,4,10,128]{0,2,3,1:T(8,128)(2,1)} copy(bf16[20,4,10,128]{3,2,1,0:T(8,128)(2,1)S(1)} %fusion.35) | data formatting | bytes 409600 | tf_op jit(solution)/shard_map/convert_element_type | solution.py:39
  24.0 0.3 broadcast_multiply_fusion.1
  24.3 0.1 copy.107
  24.5 4.3 %fusion.7 = bf16[10,10,4,128]{0,1,3,2:T(8,128)(2,1)} fusion(bf16[4,10,20,128]{2,1,3,0:T(8,128)(2,1)S(1)} %copy.114, bf16[20,4,10,128]{0,2,3,1:T(8,128)(2,1)} %copy.111, f32[10,10,128]{0,1,2:T(8,128)S(1)} %broadcast_multiply_fusion.1, f32[4,128]{1,0:T(4,128)S(1)} %slice-done, f32[10,10]{0,1:T(8,128)S(1)} %copy.107, bf16[20,20,128]{1,0,2:T(8,128)(2,1)} %copy.112), kind=kOutput, calls=%fused_computation.14 | convolution fusion | flops 6451200 | bytes 668048 | tf_op jit(solution)/shard_map/aije,jame->imae/dot_general | solution.py:45
  28.8 0.6 compare_select_fusion
  29.4 0.1 copy.116
  29.5 3.7 %copy.124 = bf16[84,84,128]{1,0,2:T(8,128)(2,1)S(1)} copy(bf16[84,84,128]{2,1,0:T(8,128)(2,1)} %param.32) | data formatting | bytes 3612672 | tf_op args[9]
  33.2 2.8 %copy.115 = bf16[10,10,512]{2,1,0:T(8,128)(2,1)S(1)} copy(bf16[10,10,512]{0,1,2:T(8,128)(2,1)} %bitcast.161) | data formatting | bytes 204800 | tf_op jit(solution)/shard_map/reshape | solution.py:80
  36.0 1.0 pad.14
  37.0 2.2 reshape.456
  39.2 0.1 slice.103
  39.3 0.1 copy.166
  39.4 0.1 div.52
  39.5 0.1 fusion.47
  39.6 0.1 slice.128
  39.7 0.1 bitcast_multiply_fusion.2
  39.8 1.6 fusion.44
  41.4 0.1 bitcast_convert_fusion
  41.5 0.7 copy.170
  42.2 0.1 copy.122
  42.3 0.1 div.59
  42.4 0.1 copy.118
  42.5 0.1 fusion.73
  42.6 10.3 %multiply_reduce_fusion = (f32[128,4,28]{0,2,1:T(8,128)S(1)}, bf16[4,28,84,128]{3,2,1,0:T(8,128)(2,1)}) fusion(f32[128,84]{0,1:T(8,128)} %copy.170, f32[84,128]{1,0:T(8,128)S(1)} %copy.122, f32[28,128]{1,0:T(8,128)S(1)} %fusion.50, f32[4,128,1,1]{0,1,3,2:T(8,128)S(1)} %bitcast.173, f32[4,4,28,84]{3,1,2,0:T(4,128)S(1)} %copy-done.1), kind=kOutput, calls=%fused_computation.10 | convolution fusion | flops 65013760 | bytes 2718720 | tf_op jit(solution)/shard_map/kaij,ke->aije/dot_general | solution.py:27
  52.9 7.7 %copy.128 = bf16[4,28,84,128]{2,1,3,0:T(8,128)(2,1)} copy(bf16[4,28,84,128]{3,2,1,0:T(8,128)(2,1)} %get-tuple-element.74) | data formatting | bytes 4816896 | tf_op jit(solution)/shard_map/convert_element_type | solution.py:30
  60.6 9.3 %fusion.4 = bf16[84,4,28,128]{3,0,2,1:T(8,128)(2,1)} fusion(f32[28,128]{1,0:T(8,128)S(1)} %fusion.50, f32[84,128]{1,0:T(8,128)S(1)} %copy.122, f32[4,128,1,1]{0,1,3,2:T(8,128)S(1)} %bitcast.172, f32[4,84,4,28]{1,2,3,0:T(4,128)S(1)} %copy-done.3), kind=kOutput, calls=%fused_computation.9 | convolution fusion | flops 61415424 | bytes 2618368 | tf_op jit(solution)/shard_map/kjai,ke->jaie/dot_general | solution.py:33
  69.9 7.7 %copy.123 = bf16[84,4,28,128]{0,2,3,1:T(8,128)(2,1)} copy(bf16[84,4,28,128]{3,0,2,1:T(8,128)(2,1)} %fusion.4) | data formatting | bytes 4816896 | tf_op jit(solution)/shard_map/convert_element_type | solution.py:39
  77.6 1.9 broadcast_multiply_fusion
  79.5 0.1 copy.117
  79.6 8.0 %fusion = bf16[28,28,4,128]{0,1,3,2:T(8,128)(2,1)} fusion(f32[28,28,128]{0,1,2:T(8,128)} %broadcast_multiply_fusion, f32[4,128]{1,0:T(4,128)S(1)} %copy.117, f32[28,28]{0,1:T(8,128)S(1)} %copy.116, bf16[4,28,84,128]{2,1,3,0:T(8,128)(2,1)} %copy.128, bf16[84,4,28,128]{0,2,3,1:T(8,128)(2,1)} %copy.123, bf16[84,84,128]{1,0,2:T(8,128)(2,1)S(1)} %copy.124), kind=kOutput, calls=%fused_computation.3 | convolution fusion | flops 272556032 | bytes 7832640 | tf_op jit(solution)/shard_map/aije,jame->imae/dot_general | solution.py:45
  87.6 5.6 %copy.129 = bf16[28,28,4,128]{3,2,1,0:T(4,128)(2,1)S(1)} copy(bf16[28,28,4,128]{0,1,3,2:T(8,128)(2,1)} %fusion) | data formatting | bytes 1605632 | tf_op jit(solution)/shard_map/convert.4
  93.2 0.1 copy.190
  93.4 0.2 fusion.28
  93.7 2.4 %copy.130 = bf16[1024,812]{1,0:T(8,128)(2,1)} copy(bf16[1024,812]{0,1:T(8,128)(2,1)S(1)} %fusion.28) | data formatting | bytes 3325952 | tf_op jit(solution)/shard_map/concatenate | solution.py:166
  96.1 6.8 %scatter_custom_fusion.1 = bf16[812,1536]{0,1:T(8,128)(2,1)S(1)} fusion(s32[1024]{0:T(1024)} %bitcast.177, bf16[1024,812]{1,0:T(8,128)(2,1)} %copy.130, bf16[]{:T(256)} %constant.124.clone.1), kind=kCustom, calls=%fused_computation.37 | custom fusion | bytes 2494976 | tf_op jit(solution)/shard_map/scatter | solution.py:75
  102.9 2.6 %all_to_all.16 = bf16[812,128,12]{0,2,1:T(8,128)(2,1)} reshape(bf16[812,1536]{0,1:T(8,128)(2,1)S(1)} %scatter_custom_fusion.1) | data formatting | bytes 4988928 | tf_op jit(solution)/shard_map/all_to_all | solution.py:168
  105.5 18.6 %all-to-all-start.1 = ((bf16[812,128,12]{0,2,1:T(8,128)(2,1)}), bf16[812,128,12]{0,2,1:T(8,128)(2,1)}, u32[]{:S(2)}, u32[]{:S(2)}) async-start(bf16[812,128,12]{0,2,1:T(8,128)(2,1)} %all_to_all.16), calls=%async_computation.1 | async-start | bytes 7340032 | tf_op jit(solution)/shard_map/all_to_all | solution.py:168
  124.2 0.7 copy.131
  124.9 85.9 %all-to-all-done.1 = bf16[812,128,12]{0,2,1:T(8,128)(2,1)} async-done(((bf16[812,128,12]{0,2,1:T(8,128)(2,1)}), bf16[812,128,12]{0,2,1:T(8,128)(2,1)}, u32[]{:S(2)}, u32[]{:S(2)}) %all-to-all-start.1) | async-done | bytes 2494496 | tf_op jit(solution)/shard_map/all_to_all | solution.py:168
  210.8 4.3 %all_to_all.18 = bf16[812,1536]{0,1:T(8,128)(2,1)S(1)} reshape(bf16[812,128,12]{0,2,1:T(8,128)(2,1)} %all-to-all-done.1) | data formatting | bytes 4988928 | tf_op jit(solution)/shard_map/all_to_all | solution.py:168
  215.1 1.6 fusion.14
  216.7 1.2 fusion.30
  217.8 0.6 pad_maximum_fusion
  218.5 0.2 fusion.21
  218.7 1.7 add.188
  (35 shorter events, 0.2 us)
Async XLA Ops:
  0.6 19.4 %copy-start.4 = (f32[12,128]{1,0:T(8,128)S(1)}, f32[12,128]{1,0:T(8,128)}, u32[]{:S(2)}) copy-start(f32[12,128]{1,0:T(8,128)} %param.24) | copy-start | bytes 18436
  5.0 34.3 %all-to-all-start = ((f32[97,4,32]{0,2,1:T(8,128)}), f32[97,4,32]{0,2,1:T(8,128)S(1)}, u32[]{:S(2)}, u32[]{:S(2)}) async-start(f32[97,4,32]{0,2,1:T(8,128)} %bitcast.9), calls=%async_computation | async-start | bytes 131072 | tf_op jit(solution)/shard_map/all_to_all | solution.py:139
  18.9 5.5 %copy-start.2 = (f32[28,28]{1,0:T(8,128)S(1)}, f32[28,28]{1,0:T(8,128)}, u32[]{:S(2)}) copy-start(f32[28,28]{1,0:T(8,128)} %param.37) | copy-start | bytes 9412
  18.9 5.6 %copy-start.5 = (s32[4,128]{1,0:T(4,128)S(1)}, s32[4,128]{1,0:T(4,128)}, u32[]{:S(2)}) copy-start(s32[4,128]{1,0:T(4,128)} %param.27) | copy-start | bytes 6148
  18.9 5.6 %copy-start.6 = (s32[4,128]{1,0:T(4,128)S(1)}, s32[4,128]{1,0:T(4,128)}, u32[]{:S(2)}) copy-start(s32[4,128]{1,0:T(4,128)} %param.33) | copy-start | bytes 6148
  18.9 5.6 %slice-start = ((f32[12,128]{1,0:T(8,128)}), f32[4,128]{1,0:T(4,128)S(1)}, s32[]{:S(2)}) async-start(f32[12,128]{1,0:T(8,128)} %param.24), calls=%async_computation.2 | async-start | bytes 4096 | tf_op jit(solution)/shard_map/slice | solution.py:46
  37.0 5.6 %copy-start.1 = (f32[4,4,28,84]{3,1,2,0:T(4,128)S(1)}, f32[4,4,28,84]{3,1,2,0:T(4,128)}, u32[]{:S(2)}) copy-start(f32[4,4,28,84]{3,1,2,0:T(4,128)} %param.35) | copy-start | bytes 451588
  52.9 7.7 %copy-start.3 = (f32[4,84,4,28]{1,2,3,0:T(4,128)S(1)}, f32[4,84,4,28]{1,2,3,0:T(4,128)}, u32[]{:S(2)}) copy-start(f32[4,84,4,28]{1,2,3,0:T(4,128)} %param.36) | copy-start | bytes 451588
  87.6 5.8 %copy-start = (bf16[784,512]{1,0:T(8,128)(2,1)S(1)}, bf16[784,512]{1,0:T(8,128)(2,1)}, u32[]{:S(2)}) copy-start(bf16[784,512]{1,0:T(8,128)(2,1)} %reshape.456) | copy-start | bytes 2408452
  105.5 105.3 %all-to-all-start.1 = ((bf16[812,128,12]{0,2,1:T(8,128)(2,1)}), bf16[812,128,12]{0,2,1:T(8,128)(2,1)}, u32[]{:S(2)}, u32[]{:S(2)}) async-start(bf16[812,128,12]{0,2,1:T(8,128)(2,1)} %all_to_all.16), calls=%async_computation.1 | async-start | bytes 7340032 | tf_op jit(solution)/shard_map/all_to_all | solution.py:168
  124.9 90.2 %copy-start.7 = (s32[1536]{0:T(1024)S(1)}, s32[1536]{0:T(1024)}, u32[]{:S(2)}) copy-start(s32[1536]{0:T(1024)} %param.34) | copy-start | bytes 18436
where the time goes:
time: 222 us; the launch traced here: 220 us
  waiting for transfers between devices  85.9 us (39%)
  local copies, waits for them, and re-layouts  61.4 us (28%)
  matrix products  39.2 us (18%)
  starting transfers between devices  22.9 us (10%)
  other arithmetic  9.99 us (4%)
    all_to_all x1, waiting for transfers between devices, on_device(): lax.all_to_all(fill_buffer(combined, positions, groups * per_owner), 'geo...  85.9 us
    all_to_all x1, starting transfers between devices, on_device(): lax.all_to_all(fill_buffer(combined, positions, groups * per_owner), 'geo...  18.6 us
    dot_general x2, matrix products, condense(): jnp.einsum('aije,jame->imae', lift_mat, solved, preferred_element_type=jn...  12.3 us
    dot_general x2, matrix products, condense(): jnp.einsum('kaij,ke->aije', lift_table, geometry[:term_count], precision=...  12 us
    dot_general x2, matrix products, condense(): jnp.einsum('kjai,ke->jaie', trace_table, geometry[term_count:2 * term_cou...  10.5 us
    convert_element_type x2, local copies, waits for them, and re-layouts, condense(): (trace_mix * inner_mask[:, None, None, :] * face_mask[None, None, :, :])....  10.4 us
    convert_element_type x2, local copies, waits for them, and re-layouts, condense(): (lift_mix * face_mask[None, :, None, :] * inner_mask[None, None, :, :]).a...  9.37 us
    unnamed x31, local copies, waits for them, and re-layouts  8.98 us
  transfers between devices with their start and end apart: 2, of which 1 were waited for; matrix products, arithmetic and copies ran while one was open for 14% of the time, Pallas kernels for 0%

commit v1 on v0

--- a/solution.py
+++ b/solution.py
@@ -165,12 +165,20 @@
     )
     combined = jnp.concatenate([embed_rows(low_rows, NF_LO, wide_face), high_rows], axis=1)
     positions = jnp.concatenate([low_target, high_target])
-    arrived_rows = lax.all_to_all(
-        fill_buffer(combined, positions, groups * per_owner),
-        "geo",
-        split_axis=1,
-        concat_axis=1,
-        tiled=True,
+    arrived_rows = jnp.concatenate(
+        lax.all_to_all(
+            jnp.stack(
+                jnp.split(
+                    fill_buffer(combined, positions, groups * per_owner),
+                    lax.axis_size("geo"),
+                    axis=1,
+                )
+            ),
+            "geo",
+            0,
+            0,
+        ),
+        axis=1,
     )
     blocks, right_side = accumulate(blocks, right_side, arrived_rows, recv_face, wide_face)
     return (low_particular, high_particular, blocks, right_side)

time: 222 us -> 297 us (1.34)
  local copies, waits for them, and re-layouts: 61.4 us -> 137 us
    unnamed x31 -> x158, local copies, waits for them, and re-layouts: 8.98 us -> 86.8 us
    all_to_all x2 -> x0, local copies, waits for them, and re-layouts: 6.91 us -> none  [on_device(): lax.all_to_all(fill_buffer(combined, positions, groups * per_owner), 'geo...]
    reshape x0 -> x1, local copies, waits for them, and re-layouts: none -> 4.28 us  [on_device(): jnp.concatenate(lax.all_to_all(jnp.stack(jnp.split(fill_buffer(combined,...]
    another operation x1 -> x2, local copies, waits for them, and re-layouts: 5.57 us -> 6.18 us
  transfers between devices with their start and end apart: 2 -> 2, of which waited for: 1 -> 1; matrix products, arithmetic and copies ran while one was open for 14% -> 10% of each run, Pallas kernels for 0% -> 0%
where the time goes in v1:
time: 297 us; the launch traced here: 296 us
  local copies, waits for them, and re-layouts  137 us (46%)
  waiting for transfers between devices  85.9 us (29%)
  matrix products  39.2 us (13%)
  starting transfers between devices  22.9 us (8%)
  other arithmetic  9.99 us (3%)
    unnamed x158, local copies, waits for them, and re-layouts  86.8 us
    all_to_all x1, waiting for transfers between devices, on_device(): lax.all_to_all(jnp.stack(jnp.split(fill_buffer(combined, positions, group...  85.9 us
    all_to_all x1, starting transfers between devices, on_device(): lax.all_to_all(jnp.stack(jnp.split(fill_buffer(combined, positions, group...  18.6 us
    dot_general x2, matrix products, condense(): jnp.einsum('aije,jame->imae', lift_mat, solved, preferred_element_type=jn...  12.3 us
    dot_general x2, matrix products, condense(): jnp.einsum('kaij,ke->aije', lift_table, geometry[:term_count], precision=...  12 us
    dot_general x2, matrix products, condense(): jnp.einsum('kjai,ke->jaie', trace_table, geometry[term_count:2 * term_cou...  10.5 us
    convert_element_type x2, local copies, waits for them, and re-layouts, condense(): (trace_mix * inner_mask[:, None, None, :] * face_mask[None, None, :, :])....  10.4 us
    convert_element_type x2, local copies, waits for them, and re-layouts, condense(): (lift_mix * face_mask[None, :, None, :] * inner_mask[None, None, :, :]).a...  9.37 us
  transfers between devices with their start and end apart: 2, of which 1 were waited for; matrix products, arithmetic and copies ran while one was open for 10% of the time, Pallas kernels for 0%

profile of v1, /device:TPU:27, one launch (start us, length us, event | category | flops | bytes accessed | tf_op | source)
XLA Modules:
  0.0 296.1 jit_solution(16014224589356669075)
XLA Ops:
  0.6 0.7 convert_element_type.120
  1.4 0.7 convert_bitcast_fusion
  2.0 0.7 maximum_bitcast_fusion
  2.8 0.7 compare_select_fusion.2
  3.5 1.5 scatter_custom_fusion
  5.0 4.3 %all-to-all-start = ((f32[97,4,32]{0,2,1:T(8,128)}), f32[97,4,32]{0,2,1:T(8,128)S(1)}, u32[]{:S(2)}, u32[]{:S(2)}) async-start(f32[97,4,32]{0,2,1:T(8,128)} %bitcast.9), calls=%async_computation | async-start | bytes 131072 | tf_op jit(solution)/shard_map/all_to_all | solution.py:139
  9.2 0.7 broadcast_multiply_fusion.2
  9.9 0.7 bitcast_convert_fusion.2
  10.6 2.2 copy.112
  12.8 1.0 multiply_reduce_fusion.2
  14.4 1.0 copy.113
  15.5 1.7 multiply_reduce_fusion.1
  17.2 1.7 copy.114
  18.9 0.9 slice.92
  20.0 1.2 fusion.35
  21.3 2.7 copy.111
  24.5 4.3 %fusion.7 = bf16[10,10,4,128]{0,1,3,2:T(8,128)(2,1)} fusion(bf16[4,10,20,128]{2,1,3,0:T(8,128)(2,1)S(1)} %copy.114, bf16[20,4,10,128]{0,2,3,1:T(8,128)(2,1)} %copy.111, f32[10,10,128]{0,1,2:T(8,128)S(1)} %broadcast_multiply_fusion.1, f32[4,128]{1,0:T(4,128)S(1)} %slice-done, f32[10,10]{0,1:T(8,128)S(1)} %copy.107, bf16[20,20,128]{1,0,2:T(8,128)(2,1)} %copy.112), kind=kOutput, calls=%fused_computation.14 | convolution fusion | flops 6451200 | bytes 668048 | tf_op jit(solution)/shard_map/aije,jame->imae/dot_general | solution.py:45
  29.5 3.7 %copy.124 = bf16[84,84,128]{1,0,2:T(8,128)(2,1)S(1)} copy(bf16[84,84,128]{2,1,0:T(8,128)(2,1)} %param.32) | data formatting | bytes 3612672 | tf_op args[9]
  33.2 2.8 copy.115
  36.0 1.0 pad.14
  37.0 2.1 reshape.460
  39.7 1.6 fusion.44
  41.4 0.7 copy.170
  42.6 10.3 %multiply_reduce_fusion = (f32[128,4,28]{0,2,1:T(8,128)S(1)}, bf16[4,28,84,128]{3,2,1,0:T(8,128)(2,1)}) fusion(f32[128,84]{0,1:T(8,128)} %copy.170, f32[84,128]{1,0:T(8,128)S(1)} %copy.122, f32[28,128]{1,0:T(8,128)S(1)} %fusion.50, f32[4,128,1,1]{0,1,3,2:T(8,128)S(1)} %bitcast.684, f32[4,4,28,84]{3,1,2,0:T(4,128)S(1)} %copy-done.1), kind=kOutput, calls=%fused_computation.10 | convolution fusion | flops 65013760 | bytes 2718720 | tf_op jit(solution)/shard_map/kaij,ke->aije/dot_general | solution.py:27
  52.9 7.7 %copy.128 = bf16[4,28,84,128]{2,1,3,0:T(8,128)(2,1)} copy(bf16[4,28,84,128]{3,2,1,0:T(8,128)(2,1)} %get-tuple-element.74) | data formatting | bytes 4816896 | tf_op jit(solution)/shard_map/convert_element_type | solution.py:30
  60.6 9.3 %fusion.4 = bf16[84,4,28,128]{3,0,2,1:T(8,128)(2,1)} fusion(f32[28,128]{1,0:T(8,128)S(1)} %fusion.50, f32[84,128]{1,0:T(8,128)S(1)} %copy.122, f32[4,128,1,1]{0,1,3,2:T(8,128)S(1)} %bitcast.683, f32[4,84,4,28]{1,2,3,0:T(4,128)S(1)} %copy-done.3), kind=kOutput, calls=%fused_computation.9 | convolution fusion | flops 61415424 | bytes 2618368 | tf_op jit(solution)/shard_map/kjai,ke->jaie/dot_general | solution.py:33
  69.9 7.7 %copy.123 = bf16[84,4,28,128]{0,2,3,1:T(8,128)(2,1)} copy(bf16[84,4,28,128]{3,0,2,1:T(8,128)(2,1)} %fusion.4) | data formatting | bytes 4816896 | tf_op jit(solution)/shard_map/convert_element_type | solution.py:39
  77.6 1.9 broadcast_multiply_fusion
  79.6 8.0 %fusion = bf16[28,28,4,128]{0,1,3,2:T(8,128)(2,1)} fusion(f32[28,28,128]{0,1,2:T(8,128)} %broadcast_multiply_fusion, f32[4,128]{1,0:T(4,128)S(1)} %copy.117, f32[28,28]{0,1:T(8,128)S(1)} %copy.116, bf16[4,28,84,128]{2,1,3,0:T(8,128)(2,1)} %copy.128, bf16[84,4,28,128]{0,2,3,1:T(8,128)(2,1)} %copy.123, bf16[84,84,128]{1,0,2:T(8,128)(2,1)S(1)} %copy.124), kind=kOutput, calls=%fused_computation.3 | convolution fusion | flops 272556032 | bytes 7832640 | tf_op jit(solution)/shard_map/aije,jame->imae/dot_general | solution.py:45
  87.6 5.6 %copy.129 = bf16[28,28,4,128]{3,2,1,0:T(4,128)(2,1)S(1)} copy(bf16[28,28,4,128]{0,1,3,2:T(8,128)(2,1)} %fusion) | data formatting | bytes 1605632 | tf_op jit(solution)/shard_map/convert.4
  93.6 2.4 copy.130
  96.1 6.8 %scatter_custom_fusion.1 = bf16[812,1536]{0,1:T(8,128)(2,1)S(1)} fusion(s32[1024]{0:T(1024)} %bitcast.688, bf16[1024,812]{1,0:T(8,128)(2,1)} %copy.130, bf16[]{:T(256)} %constant.124.clone.1), kind=kCustom, calls=%fused_computation.37 | custom fusion | bytes 2494976 | tf_op jit(solution)/shard_map/scatter | solution.py:75
  108.3 0.6 constant_dynamic-update-slice_fusion.118
  111.4 0.6 constant_dynamic-update-slice_fusion.113
  113.3 0.6 constant_dynamic-update-slice_fusion.110
  118.1 0.6 constant_dynamic-update-slice_fusion.102
  123.0 0.6 constant_dynamic-update-slice_fusion.94
  126.7 0.6 constant_dynamic-update-slice_fusion.88
  127.3 0.6 constant_dynamic-update-slice_fusion.87
  127.9 0.6 constant_dynamic-update-slice_fusion.86
  131.6 0.6 constant_dynamic-update-slice_fusion.80
  132.8 0.6 constant_dynamic-update-slice_fusion.78
  136.5 0.6 constant_dynamic-update-slice_fusion.72
  137.8 0.6 constant_dynamic-update-slice_fusion.70
  140.2 0.6 constant_dynamic-update-slice_fusion.66
  141.4 0.6 constant_dynamic-update-slice_fusion.64
  142.7 0.6 constant_dynamic-update-slice_fusion.62
  145.2 0.6 constant_dynamic-update-slice_fusion.58
  146.4 0.6 constant_dynamic-update-slice_fusion.56
  151.3 0.6 constant_dynamic-update-slice_fusion.48
  152.5 0.6 constant_dynamic-update-slice_fusion.46
  156.2 0.6 constant_dynamic-update-slice_fusion.40
  166.0 0.6 constant_dynamic-update-slice_fusion.24
  170.9 0.6 constant_dynamic-update-slice_fusion.16
  174.6 0.6 constant_dynamic-update-slice_fusion.10
  177.0 0.6 constant_dynamic-update-slice_fusion.6
  181.3 18.6 %all-to-all-start.1 = ((bf16[128,812,12]{1,2,0:T(8,128)(2,1)}), bf16[128,812,12]{1,2,0:T(8,128)(2,1)}, u32[]{:S(2)}, u32[]{:S(2)}) async-start(bf16[128,812,12]{1,2,0:T(8,128)(2,1)} %constant_dynamic-update-slice_fusion), calls=%async_computation.1 | async-start | bytes 7340032 | tf_op jit(solution)/shard_map/all_to_all | solution.py:169
  200.0 0.7 copy.131
  200.7 85.9 %all-to-all-done.1 = bf16[128,812,12]{1,2,0:T(8,128)(2,1)} async-done(((bf16[128,812,12]{1,2,0:T(8,128)(2,1)}), bf16[128,812,12]{1,2,0:T(8,128)(2,1)}, u32[]{:S(2)}, u32[]{:S(2)}) %all-to-all-start.1) | async-done | bytes 2494496 | tf_op jit(solution)/shard_map/all_to_all | solution.py:169
  286.6 4.3 %reshape.465 = bf16[812,1536]{0,1:T(8,128)(2,1)S(1)} reshape(bf16[812,128,12]{0,2,1:T(8,128)(2,1)} %bitcast.175) | data formatting | bytes 4988928 | tf_op jit(solution)/shard_map/reshape | solution.py:168
  290.9 1.6 fusion.14
  292.5 1.2 fusion.30
  293.7 0.6 pad_maximum_fusion
  294.5 1.7 add.188
  (162 shorter events, 67.4 us)
Async XLA Ops:
  0.6 19.4 %copy-start.4 = (f32[12,128]{1,0:T(8,128)S(1)}, f32[12,128]{1,0:T(8,128)}, u32[]{:S(2)}) copy-start(f32[12,128]{1,0:T(8,128)} %param.24) | copy-start | bytes 18436
  5.0 34.2 %all-to-all-start = ((f32[97,4,32]{0,2,1:T(8,128)}), f32[97,4,32]{0,2,1:T(8,128)S(1)}, u32[]{:S(2)}, u32[]{:S(2)}) async-start(f32[97,4,32]{0,2,1:T(8,128)} %bitcast.9), calls=%async_computation | async-start | bytes 131072 | tf_op jit(solution)/shard_map/all_to_all | solution.py:139
  15.5 8.8 %copy-start.2 = (f32[28,28]{1,0:T(8,128)S(1)}, f32[28,28]{1,0:T(8,128)}, u32[]{:S(2)}) copy-start(f32[28,28]{1,0:T(8,128)} %param.37) | copy-start | bytes 9412
  17.2 7.2 %copy-start.5 = (s32[4,128]{1,0:T(4,128)S(1)}, s32[4,128]{1,0:T(4,128)}, u32[]{:S(2)}) copy-start(s32[4,128]{1,0:T(4,128)} %param.27) | copy-start | bytes 6148
  17.2 7.3 %copy-start.6 = (s32[4,128]{1,0:T(4,128)S(1)}, s32[4,128]{1,0:T(4,128)}, u32[]{:S(2)}) copy-start(s32[4,128]{1,0:T(4,128)} %param.33) | copy-start | bytes 6148
  17.2 7.3 %slice-start = ((f32[12,128]{1,0:T(8,128)}), f32[4,128]{1,0:T(4,128)S(1)}, s32[]{:S(2)}) async-start(f32[12,128]{1,0:T(8,128)} %param.24), calls=%async_computation.2 | async-start | bytes 4096 | tf_op jit(solution)/shard_map/slice | solution.py:46
  36.0 6.6 %copy-start.1 = (f32[4,4,28,84]{3,1,2,0:T(4,128)S(1)}, f32[4,4,28,84]{3,1,2,0:T(4,128)}, u32[]{:S(2)}) copy-start(f32[4,4,28,84]{3,1,2,0:T(4,128)} %param.35) | copy-start | bytes 451588
  52.9 7.7 %copy-start.3 = (f32[4,84,4,28]{1,2,3,0:T(4,128)S(1)}, f32[4,84,4,28]{1,2,3,0:T(4,128)}, u32[]{:S(2)}) copy-start(f32[4,84,4,28]{1,2,3,0:T(4,128)} %param.36) | copy-start | bytes 451588
  87.6 5.8 %copy-start = (bf16[784,512]{1,0:T(8,128)(2,1)S(1)}, bf16[784,512]{1,0:T(8,128)(2,1)}, u32[]{:S(2)}) copy-start(bf16[784,512]{1,0:T(8,128)(2,1)} %reshape.460) | copy-start | bytes 2408452
  181.3 105.3 %all-to-all-start.1 = ((bf16[128,812,12]{1,2,0:T(8,128)(2,1)}), bf16[128,812,12]{1,2,0:T(8,128)(2,1)}, u32[]{:S(2)}, u32[]{:S(2)}) async-start(bf16[128,812,12]{1,2,0:T(8,128)(2,1)} %constant_dynamic-update-slice_fusion), calls=%async_computation.1 | async-start | bytes 7340032 | tf_op jit(solution)/shard_map/all_to_all | solution.py:169
  200.0 90.9 %copy-start.7 = (s32[1536]{0:T(1024)S(1)}, s32[1536]{0:T(1024)}, u32[]{:S(2)}) copy-start(s32[1536]{0:T(1024)} %param.34) | copy-start | bytes 18436
